TPU v7x, 32 devices: a whole 2x2x4 slice. The times are simulated.
32 devices in a mesh: row: 8 (over y, x, core), col: 4 (over z).
Axes of the slice: x: 2, y: 2, z: 4, core: 2. Of those that a mesh axis runs over, the one named last changes fastest.
Arguments:
- coeffs: bfloat16 [16384, 2048], P('row', 'col'), may hold values from -0.8984375 to 0.8984375
- occupations: float32 [2048], replicated, may hold values from 0.05 to 2
- block_order: int32 [32], replicated, may hold values from 0 to 31, as said below
- neighbours: int32 [32, 15], P(('row', 'col')), may hold values from 0 to 31, as said below
- counts: int32 [32], P(('row', 'col')), may hold values from 4 to 15, as said below
Outputs:
- density: bfloat16 [32, 15, 512, 512], P(('row', 'col'))
Inputs may be any that keep to these rules, and one draw needn't show every extreme that they name: Within each aligned group of 4 entries, block_order is a permutation of that group's own indices. For atom row block a, the first counts[a] entries of neighbours[a] are distinct blocks b with |b - a| < 8; the remaining entries equal a. `counts`: some block has 15 live slots in every draw.
All inputs are finite; a program needn't handle non-finite values.
Results may differ from a plain program's by a relative error of at most 0.0044.
Values may be sent and summed in bfloat16 or wider, within the bound.
A program may use at most 128 MiB of HBM per device.

v0:
```python
import jax
import jax.numpy as jnp
from jax import lax
from jax.sharding import PartitionSpec as P

W = 8
NNB = 15


def from_behind(block, axis, distance):
    devices = range(lax.axis_size(axis))
    route = [(i - distance, i) for i in devices if i - distance in devices]
    return lax.ppermute(block, axis, route)


def shards(coeffs, occupations, block_order, neighbours, counts):
    col_count = lax.axis_size("col")
    states_local = coeffs.shape[1]
    block_rows = coeffs.shape[0] // col_count
    group_base = lax.axis_index("row") * col_count
    own_index = group_base + lax.axis_index("col")
    local_blocks = coeffs.reshape(col_count, block_rows, states_local)
    picks = lax.dynamic_slice_in_dim(block_order, group_base, col_count) - group_base
    outgoing = local_blocks[picks]
    own_block = lax.all_to_all(outgoing, "col", split_axis=0, concat_axis=2, tiled=True)
    downward = own_block
    step = 1
    while step < W:
        received = from_behind(downward, ("row", "col"), step)
        downward = jnp.concatenate([downward, received], axis=0)
        step = step * 2
    upward = own_block
    step = 1
    while step < W:
        received = from_behind(upward, ("row", "col"), -step)
        upward = jnp.concatenate([upward, received], axis=0)
        step = step * 2
    window = jnp.concatenate([downward[1:][::-1], upward], axis=0)
    weighted = (own_block[0].astype(jnp.float32) * occupations[None, :]).astype(jnp.bfloat16)
    offsets = neighbours[0] - own_index + (W - 1)
    live_count = counts[0]
    chosen = window[offsets]
    products = jnp.einsum("ik,jnk->jin", weighted, chosen, preferred_element_type=jnp.float32)
    slots = jnp.arange(NNB, dtype=jnp.int32)
    live = (slots < live_count)[:, None, None]
    result = jnp.where(live, products, 0.0).astype(jnp.bfloat16)
    return result[None]


def solution(mesh):
    return jax.shard_map(
        shards,
        mesh=mesh,
        in_specs=(P("row", "col"), P(), P(), P(("row", "col"), None), P(("row", "col"))),
        out_specs=P(("row", "col"), None, None, None),
        check_vma=False,
    )
```

profile of v0, /device:TPU:4, one launch (start us, length us, event | category | flops | bytes accessed | tf_op | source)
XLA Modules:
  0.0 819.4 jit_solution(5868224025195781986)
XLA Ops:
  0.0 0.0 copy-start
  0.0 0.9 compare_select_fusion.1
  0.9 0.7 copy-done
  1.6 2.0 gather_fusion
  3.6 53.1 %all_to_all.18 = bf16[4,512,512]{2,1,0:T(8,128)(2,1)S(1)} all-to-all(bf16[4,512,512]{2,1,0:T(8,128)(2,1)} %gather_fusion), channel_id=1, replica_groups=mesh['row'=8,'col'=4] {'col'}, dimensions={0} | all-to-all | bytes 4194304 | tf_op jit(solution)/shard_map/all_to_all | solution.py:25
  56.7 2.7 copy.19
  59.3 0.0 copy-done.2
  59.3 2.9 copy.20
  62.3 2.1 collective-permute-start
  64.4 7.0 collective-permute-start.3
  71.4 44.3 %collective-permute-done = bf16[1,512,2048]{2,1,0:T(8,128)(2,1)S(1)} collective-permute-done((bf16[1,512,2048]{2,1,0:T(8,128)(2,1)S(1)}, bf16[1,512,2048]{2,1,0:T(8,128)(2,1)S(1)}, u32[]{:S(2)}, u32[]{:S(2)}) %collective-permute-start) | collective-permute-done | bytes 2097184 | tf_op jit(solution)/shard_map/ppermute | solution.py:13
  115.7 41.6 %collective-permute-done.3 = bf16[1,512,2048]{2,1,0:T(8,128)(2,1)S(1)} collective-permute-done((bf16[1,512,2048]{2,1,0:T(8,128)(2,1)S(1)}, bf16[1,512,2048]{2,1,0:T(8,128)(2,1)S(1)}, u32[]{:S(2)}, u32[]{:S(2)}) %collective-permute-start.3) | collective-permute-done | bytes 2097184 | tf_op jit(solution)/shard_map/ppermute | solution.py:13
  157.3 0.7 pad_maximum_fusion.3
  158.0 1.9 collective-permute-start.1
  159.9 0.0 copy-start.11
  159.9 6.3 collective-permute-start.4
  166.3 268.8 %collective-permute-done.1 = bf16[2,512,2048]{2,1,0:T(8,128)(2,1)S(1)} collective-permute-done((bf16[2,512,2048]{2,1,0:T(8,128)(2,1)S(1)}, bf16[2,512,2048]{2,1,0:T(8,128)(2,1)S(1)}, u32[]{:S(2)}, u32[]{:S(2)}) %collective-permute-start.1) | collective-permute-done | bytes 4194336 | tf_op jit(solution)/shard_map/ppermute | solution.py:13
  435.0 86.1 %collective-permute-done.4 = bf16[2,512,2048]{2,1,0:T(8,128)(2,1)S(1)} collective-permute-done((bf16[2,512,2048]{2,1,0:T(8,128)(2,1)S(1)}, bf16[2,512,2048]{2,1,0:T(8,128)(2,1)S(1)}, u32[]{:S(2)}, u32[]{:S(2)}) %collective-permute-start.4) | collective-permute-done | bytes 4194336 | tf_op jit(solution)/shard_map/ppermute | solution.py:13
  521.1 6.8 fusion.7
  527.9 0.0 copy-done.3
  528.0 0.0 copy-done.4
  528.0 0.0 copy-done.6
  528.0 0.3 copy-done.8
  528.2 2.0 collective-permute-start.2
  530.3 4.9 collective-permute-start.5
  535.8 0.0 copy-done.11
  535.8 4.1 bitcast_convert_fusion
  540.0 5.3 copy.27
  545.3 0.0 copy-done.10
  545.3 4.0 fusion.11
  549.3 161.5 %collective-permute-done.2 = bf16[4,512,2048]{2,1,0:T(8,128)(2,1)} collective-permute-done((bf16[4,512,2048]{2,1,0:T(8,128)(2,1)}, bf16[4,512,2048]{2,1,0:T(8,128)(2,1)}, u32[]{:S(2)}, u32[]{:S(2)}) %collective-permute-start.2) | collective-permute-done | bytes 8388640 | tf_op jit(solution)/shard_map/ppermute | solution.py:13
  710.8 0.0 copy-done.7
  710.8 6.4 pad_maximum_fusion
  717.3 0.0 copy-start.5
  717.3 6.0 reverse_dynamic-update-slice_fusion
  723.3 1.6 constant_dynamic-update-slice_fusion.3
  724.8 0.0 copy-done.5
  724.8 1.5 constant_dynamic-update-slice_fusion.2
  726.3 0.7 copy-done.9
  727.0 2.3 constant_dynamic-update-slice_fusion.1
  729.3 0.0 collective-permute-done.5
  729.3 8.4 %constant_dynamic-update-slice_fusion = bf16[15,512,2048]{2,1,0:T(8,128)(2,1)} fusion(bf16[15,512,2048]{2,1,0:T(8,128)(2,1)} %constant_dynamic-update-slice_fusion.1, bf16[4,512,2048]{2,1,0:T(8,128)(2,1)} %collective-permute-done.5), kind=kLoop, calls=%fused_computation.20 | loop fusion | bytes 16777216 | tf_op jit(solution)/shard_map/concatenate | solution.py:38
  737.7 23.1 %fusion.15 = (bf16[15,512,1024]{2,1,0:T(8,128)(2,1)}, bf16[15,512,1024]{2,1,0:T(8,128)(2,1)}) fusion(bf16[15,512,2048]{2,1,0:T(8,128)(2,1)} %constant_dynamic-update-slice_fusion), kind=kLoop, calls=%fused_computation.32 | loop fusion | bytes 62914560 | tf_op jit(solution)/shard_map/gather | solution.py:42
  760.8 12.4 %gather_fusion.1 = bf16[15,512,1024]{2,1,0:T(8,128)(2,1)} fusion(bf16[15,512,1024]{2,1,0:T(8,128)(2,1)} %get-tuple-element.5, s32[1024]{0:T(1024)S(1)} %pad_clamp_fusion), kind=kCustom, calls=%fused_computation.1 | custom fusion | bytes 31457340 | tf_op jit(solution)/shard_map/gather | solution.py:42
  773.2 12.5 %gather_fusion.2 = bf16[15,512,1024]{2,1,0:T(8,128)(2,1)} fusion(bf16[15,512,1024]{2,1,0:T(8,128)(2,1)} %get-tuple-element.6, s32[1024]{0:T(1024)S(1)} %pad_clamp_fusion), kind=kCustom, calls=%fused_computation.2 | custom fusion | bytes 31457340 | tf_op jit(solution)/shard_map/gather | solution.py:42
  785.7 23.1 %fusion.8 = bf16[1,15,512,512]{2,3,1,0:T(8,128)(2,1)} fusion(bf16[15,512,1024]{2,1,0:T(8,128)(2,1)} %gather_fusion.2, bf16[15,512,1024]{2,1,0:T(8,128)(2,1)} %gather_fusion.1, pred[15]{0:T(512)(128)(4,1)S(1)} %iota_compare_fusion, bf16[512,2048]{0,1:T(8,128)(2,1)} %fusion.11), kind=kOutput, calls=%fused_computation.14 | convolution fusion | flops 16176906240 | bytes 41418768 | tf_op jit(solution)/shard_map/ik,jnk->jin/dot_general | solution.py:43
  808.8 10.6 %copy.29 = bf16[1,15,512,512]{3,2,1,0:T(8,128)(2,1)} copy(bf16[1,15,512,512]{2,3,1,0:T(8,128)(2,1)} %fusion.8) | data formatting | bytes 15728640 | tf_op jit(solution)/shard_map/broadcast_in_dim | solution.py:47
  819.4 0.0 copy-done.1
  (13 shorter events, 0.0 us)
Async XLA Ops:
  0.0 1.6 copy-start
  56.7 2.7 copy-start.2
  62.3 53.4 %collective-permute-start = (bf16[1,512,2048]{2,1,0:T(8,128)(2,1)S(1)}, bf16[1,512,2048]{2,1,0:T(8,128)(2,1)S(1)}, u32[]{:S(2)}, u32[]{:S(2)}) collective-permute-start(bf16[1,512,2048]{2,1,0:T(8,128)(2,1)S(1)} %copy.20), channel_id=1, source_target_pairs={{0,1},{1,2},{2,3},{3,4},{4,5},{5,6},{6,7},{7,8},{8,9},{9,10},{10,1... | collective-permute-start | bytes 6291464 | tf_op jit(solution)/shard_map/ppermute | solution.py:13
  64.4 92.9 %collective-permute-start.3 = (bf16[1,512,2048]{2,1,0:T(8,128)(2,1)S(1)}, bf16[1,512,2048]{2,1,0:T(8,128)(2,1)S(1)}, u32[]{:S(2)}, u32[]{:S(2)}) collective-permute-start(bf16[1,512,2048]{2,1,0:T(8,128)(2,1)S(1)} %copy.20), channel_id=1, source_target_pairs={{1,0},{2,1},{3,2},{4,3},{5,4},{6,5},{7,6},{8,7},{9,8},{10,9},{11,1... | collective-permute-start | bytes 6291464 | tf_op jit(solution)/shard_map/ppermute | solution.py:13
  115.7 412.2 %copy-start.3 = (bf16[1,512,2048]{2,1,0:T(8,128)(2,1)}, bf16[1,512,2048]{2,1,0:T(8,128)(2,1)S(1)}, u32[]{:S(2)}) copy-start(bf16[1,512,2048]{2,1,0:T(8,128)(2,1)S(1)} %collective-permute-done) | copy-start | bytes 6291460
  157.3 370.6 %copy-start.4 = (bf16[1,512,2048]{2,1,0:T(8,128)(2,1)}, bf16[1,512,2048]{2,1,0:T(8,128)(2,1)S(1)}, u32[]{:S(2)}) copy-start(bf16[1,512,2048]{2,1,0:T(8,128)(2,1)S(1)} %collective-permute-done.3) | copy-start | bytes 6291460
  158.0 277.0 %collective-permute-start.1 = (bf16[2,512,2048]{2,1,0:T(8,128)(2,1)S(1)}, bf16[2,512,2048]{2,1,0:T(8,128)(2,1)S(1)}, u32[]{:S(2)}, u32[]{:S(2)}) collective-permute-start(bf16[2,512,2048]{2,1,0:T(8,128)(2,1)S(1)} %get-tuple-element.10), channel_id=1, source_target_pairs={{0,2},{1,3},{2,4},{3,5},{4,6},{5,7},{6,8},{7,9},{8,10},{9,11},{10,... | collective-permute-start | bytes 12582920 | tf_op jit(solution)/shard_map/ppermute | solution.py:13
  159.9 375.9 %copy-start.11 = (s32[1,15]{1,0:T(1,128)S(1)}, s32[1,15]{1,0:T(1,128)}, u32[]{:S(2)}) copy-start(s32[1,15]{1,0:T(1,128)} %param.8) | copy-start | bytes 184
  159.9 361.2 %collective-permute-start.4 = (bf16[2,512,2048]{2,1,0:T(8,128)(2,1)S(1)}, bf16[2,512,2048]{2,1,0:T(8,128)(2,1)S(1)}, u32[]{:S(2)}, u32[]{:S(2)}) collective-permute-start(bf16[2,512,2048]{2,1,0:T(8,128)(2,1)S(1)} %get-tuple-element.9), channel_id=1, source_target_pairs={{2,0},{3,1},{4,2},{5,3},{6,4},{7,5},{8,6},{9,7},{10,8},{11,9},{12,... | collective-permute-start | bytes 12582920 | tf_op jit(solution)/shard_map/ppermute | solution.py:13
  435.0 92.9 %copy-start.6 = (bf16[2,512,2048]{2,1,0:T(8,128)(2,1)}, bf16[2,512,2048]{2,1,0:T(8,128)(2,1)S(1)}, u32[]{:S(2)}) copy-start(bf16[2,512,2048]{2,1,0:T(8,128)(2,1)S(1)} %collective-permute-done.1) | copy-start | bytes 12582916
  521.1 7.1 copy-start.8
  528.2 17.0 %copy-start.10 = (f32[2048]{0:T(1024)S(1)}, f32[2048]{0:T(1024)}, u32[]{:S(2)}) copy-start(f32[2048]{0:T(1024)} %param.6) | copy-start | bytes 24580
  528.2 182.6 %collective-permute-start.2 = (bf16[4,512,2048]{2,1,0:T(8,128)(2,1)}, bf16[4,512,2048]{2,1,0:T(8,128)(2,1)}, u32[]{:S(2)}, u32[]{:S(2)}) collective-permute-start(bf16[4,512,2048]{2,1,0:T(8,128)(2,1)} %get-tuple-element.8), channel_id=1, source_target_pairs={{0,4},{1,5},{2,6},{3,7},{4,8},{5,9},{6,10},{7,11},{8,12},{9,13},{1... | collective-permute-start | bytes 25165832 | tf_op jit(solution)/shard_map/ppermute | solution.py:13
  530.3 199.0 %collective-permute-start.5 = (bf16[4,512,2048]{2,1,0:T(8,128)(2,1)}, bf16[4,512,2048]{2,1,0:T(8,128)(2,1)}, u32[]{:S(2)}, u32[]{:S(2)}) collective-permute-start(bf16[4,512,2048]{2,1,0:T(8,128)(2,1)} %get-tuple-element.7), channel_id=1, source_target_pairs={{4,0},{5,1},{6,2},{7,3},{8,4},{9,5},{10,6},{11,7},{12,8},{13,9},{1... | collective-permute-start | bytes 25165832 | tf_op jit(solution)/shard_map/ppermute | solution.py:13
  545.3 165.6 %copy-start.7 = (bf16[2,512,2048]{2,1,0:T(8,128)(2,1)S(1)}, bf16[2,512,2048]{2,1,0:T(8,128)(2,1)}, u32[]{:S(2)}) copy-start(bf16[2,512,2048]{2,1,0:T(8,128)(2,1)} %copy-done.6) | copy-start | bytes 12582916
  717.3 7.6 copy-start.5
  723.3 3.7 copy-start.9
  785.7 33.8 %copy-start.1 = (bf16[2048,512]{1,0:T(8,128)(2,1)S(1)}, bf16[2048,512]{1,0:T(8,128)(2,1)}, u32[]{:S(2)}) copy-start(bf16[2048,512]{1,0:T(8,128)(2,1)} %param.5) | copy-start | bytes 6291460
where the time goes:
time: 821 us; the launch traced here: 819 us
  waiting for transfers between devices  602 us (73%)
  local copies, waits for them, and re-layouts  92.9 us (11%)
  blocking collectives  53.1 us (6%)
  starting transfers between devices  24.3 us (3%)
  matrix products  23.1 us (3%)
  other arithmetic  22.9 us (3%)
    ppermute x6, waiting for transfers between devices, from_behind(): return lax.ppermute(block, axis, route)  602 us
    all_to_all x1, blocking collectives, shards(): lax.all_to_all(outgoing, 'col', split_axis=0, concat_axis=2, tiled=True)  53.1 us
    gather x3, local copies, waits for them, and re-layouts, shards(): chosen = window[offsets]  48 us
    ppermute x6, starting transfers between devices, from_behind(): return lax.ppermute(block, axis, route)  24.3 us
    dot_general x1, matrix products, shards(): jnp.einsum('ik,jnk->jin', weighted, chosen, preferred_element_type=jnp.fl...  23.1 us
  transfers between devices with their start and end apart: 6, of which 5 were waited for; matrix products, arithmetic and copies ran while one was open for 4% of the time, Pallas kernels for 0%

commit v1 on v0

--- a/solution.py
+++ b/solution.py
@@ -22,7 +22,10 @@
     local_blocks = coeffs.reshape(col_count, block_rows, states_local)
     picks = lax.dynamic_slice_in_dim(block_order, group_base, col_count) - group_base
     outgoing = local_blocks[picks]
-    own_block = lax.all_to_all(outgoing, "col", split_axis=0, concat_axis=2, tiled=True)
+    own_block = jnp.concatenate(
+        lax.all_to_all(jnp.stack(jnp.split(outgoing, lax.axis_size("col"), axis=0)), "col", 0, 0),
+        axis=2,
+    )
     downward = own_block
     step = 1
     while step < W:

time: 821 us -> 822 us (level)
  no operation moved by 1% of the time
where the time goes in v1:
time: 822 us; the launch traced here: 821 us
  waiting for transfers between devices  602 us (73%)
  local copies, waits for them, and re-layouts  94.5 us (11%)
  blocking collectives  52.9 us (6%)
  starting transfers between devices  24.3 us (3%)
  other arithmetic  23.2 us (3%)
  matrix products  23.1 us (3%)
    ppermute x6, waiting for transfers between devices, from_behind(): return lax.ppermute(block, axis, route)  602 us
    all_to_all x1, blocking collectives, shards(): lax.all_to_all(jnp.stack(jnp.split(outgoing, lax.axis_size('col'), axis=0...  52.9 us
    gather x3, local copies, waits for them, and re-layouts, shards(): chosen = window[offsets]  48 us
    ppermute x6, starting transfers between devices, from_behind(): return lax.ppermute(block, axis, route)  24.3 us
    dot_general x1, matrix products, shards(): jnp.einsum('ik,jnk->jin', weighted, chosen, preferred_element_type=jnp.fl...  23.1 us
  transfers between devices with their start and end apart: 6, of which 5 were waited for; matrix products, arithmetic and copies ran while one was open for 4% of the time, Pallas kernels for 0%

profile of v1, /device:TPU:4, one launch (start us, length us, event | category | flops | bytes accessed | tf_op | source)
XLA Modules:
  0.0 821.1 jit_solution(6784026010760056294)
XLA Ops:
  0.0 0.0 copy-start
  0.0 0.9 compare_select_fusion.1
  0.9 0.7 copy-done
  1.6 2.0 gather_fusion
  3.6 1.7 slice_bitcast_fusion.3
  5.3 0.3 pad_maximum_fusion.5
  5.5 52.9 %all_to_all.5 = bf16[4,1,512,512]{3,2,1,0:T(8,128)(2,1)S(1)} all-to-all(bf16[4,1,512,512]{3,2,1,0:T(8,128)(2,1)S(1)} %pad_maximum_fusion.5), channel_id=1, replica_groups=mesh['row'=8,'col'=4] {'col'}, dimensions={0} | all-to-all | bytes 4194304 | tf_op jit(solution)/shard_map/all_to_all | solution.py:26
  58.4 2.7 copy.22
  61.1 0.0 copy-done.2
  61.1 2.9 copy.23
  64.0 2.1 collective-permute-start
  66.1 7.0 collective-permute-start.3
  73.2 44.3 %collective-permute-done = bf16[1,512,2048]{2,1,0:T(8,128)(2,1)S(1)} collective-permute-done((bf16[1,512,2048]{2,1,0:T(8,128)(2,1)S(1)}, bf16[1,512,2048]{2,1,0:T(8,128)(2,1)S(1)}, u32[]{:S(2)}, u32[]{:S(2)}) %collective-permute-start) | collective-permute-done | bytes 2097184 | tf_op jit(solution)/shard_map/ppermute | solution.py:13
  117.4 41.6 %collective-permute-done.3 = bf16[1,512,2048]{2,1,0:T(8,128)(2,1)S(1)} collective-permute-done((bf16[1,512,2048]{2,1,0:T(8,128)(2,1)S(1)}, bf16[1,512,2048]{2,1,0:T(8,128)(2,1)S(1)}, u32[]{:S(2)}, u32[]{:S(2)}) %collective-permute-start.3) | collective-permute-done | bytes 2097184 | tf_op jit(solution)/shard_map/ppermute | solution.py:13
  159.1 0.7 pad_maximum_fusion.3
  159.7 1.9 collective-permute-start.1
  161.6 0.0 copy-start.11
  161.7 6.3 collective-permute-start.4
  168.0 268.8 %collective-permute-done.1 = bf16[2,512,2048]{2,1,0:T(8,128)(2,1)S(1)} collective-permute-done((bf16[2,512,2048]{2,1,0:T(8,128)(2,1)S(1)}, bf16[2,512,2048]{2,1,0:T(8,128)(2,1)S(1)}, u32[]{:S(2)}, u32[]{:S(2)}) %collective-permute-start.1) | collective-permute-done | bytes 4194336 | tf_op jit(solution)/shard_map/ppermute | solution.py:13
  436.8 86.1 %collective-permute-done.4 = bf16[2,512,2048]{2,1,0:T(8,128)(2,1)S(1)} collective-permute-done((bf16[2,512,2048]{2,1,0:T(8,128)(2,1)S(1)}, bf16[2,512,2048]{2,1,0:T(8,128)(2,1)S(1)}, u32[]{:S(2)}, u32[]{:S(2)}) %collective-permute-start.4) | collective-permute-done | bytes 4194336 | tf_op jit(solution)/shard_map/ppermute | solution.py:13
  522.9 6.8 fusion.7
  529.7 0.0 copy-done.3
  529.7 0.0 copy-done.4
  529.7 0.0 copy-done.6
  529.7 0.3 copy-done.8
  529.9 2.0 collective-permute-start.2
  532.0 4.9 collective-permute-start.5
  537.5 0.0 copy-done.11
  537.6 4.1 bitcast_convert_fusion
  541.7 5.3 copy.30
  547.0 0.0 copy-done.10
  547.0 4.0 fusion.11
  551.0 161.5 %collective-permute-done.2 = bf16[4,512,2048]{2,1,0:T(8,128)(2,1)} collective-permute-done((bf16[4,512,2048]{2,1,0:T(8,128)(2,1)}, bf16[4,512,2048]{2,1,0:T(8,128)(2,1)}, u32[]{:S(2)}, u32[]{:S(2)}) %collective-permute-start.2) | collective-permute-done | bytes 8388640 | tf_op jit(solution)/shard_map/ppermute | solution.py:13
  712.5 0.0 copy-done.7
  712.5 6.4 pad_maximum_fusion
  719.0 6.0 reverse_dynamic-update-slice_fusion
  725.0 1.6 constant_dynamic-update-slice_fusion.3
  726.5 0.0 copy-done.5
  726.5 1.5 constant_dynamic-update-slice_fusion.2
  728.0 0.6 copy-done.9
  728.7 2.3 constant_dynamic-update-slice_fusion.1
  731.0 0.0 collective-permute-done.5
  731.0 8.4 %constant_dynamic-update-slice_fusion = bf16[15,512,2048]{2,1,0:T(8,128)(2,1)} fusion(bf16[15,512,2048]{2,1,0:T(8,128)(2,1)} %constant_dynamic-update-slice_fusion.1, bf16[4,512,2048]{2,1,0:T(8,128)(2,1)} %collective-permute-done.5), kind=kLoop, calls=%fused_computation.25 | loop fusion | bytes 16777216 | tf_op jit(solution)/shard_map/concatenate | solution.py:41
  739.4 23.1 %fusion.15 = (bf16[15,512,1024]{2,1,0:T(8,128)(2,1)}, bf16[15,512,1024]{2,1,0:T(8,128)(2,1)}) fusion(bf16[15,512,2048]{2,1,0:T(8,128)(2,1)} %constant_dynamic-update-slice_fusion), kind=kLoop, calls=%fused_computation.37 | loop fusion | bytes 62914560 | tf_op jit(solution)/shard_map/gather | solution.py:45
  762.5 12.4 %gather_fusion.1 = bf16[15,512,1024]{2,1,0:T(8,128)(2,1)} fusion(bf16[15,512,1024]{2,1,0:T(8,128)(2,1)} %get-tuple-element.5, s32[1024]{0:T(1024)S(1)} %pad_clamp_fusion), kind=kCustom, calls=%fused_computation.1 | custom fusion | bytes 31457340 | tf_op jit(solution)/shard_map/gather | solution.py:45
  774.9 12.5 %gather_fusion.2 = bf16[15,512,1024]{2,1,0:T(8,128)(2,1)} fusion(bf16[15,512,1024]{2,1,0:T(8,128)(2,1)} %get-tuple-element.6, s32[1024]{0:T(1024)S(1)} %pad_clamp_fusion), kind=kCustom, calls=%fused_computation.2 | custom fusion | bytes 31457340 | tf_op jit(solution)/shard_map/gather | solution.py:45
  787.4 23.1 %fusion.8 = bf16[1,15,512,512]{2,3,1,0:T(8,128)(2,1)} fusion(bf16[15,512,1024]{2,1,0:T(8,128)(2,1)} %gather_fusion.2, bf16[15,512,1024]{2,1,0:T(8,128)(2,1)} %gather_fusion.1, pred[15]{0:T(512)(128)(4,1)S(1)} %iota_compare_fusion, bf16[512,2048]{0,1:T(8,128)(2,1)} %fusion.11), kind=kOutput, calls=%fused_computation.14 | convolution fusion | flops 16176906240 | bytes 41418768 | tf_op jit(solution)/shard_map/ik,jnk->jin/dot_general | solution.py:46
  810.5 10.6 %copy.32 = bf16[1,15,512,512]{3,2,1,0:T(8,128)(2,1)} copy(bf16[1,15,512,512]{2,3,1,0:T(8,128)(2,1)} %fusion.8) | data formatting | bytes 15728640 | tf_op jit(solution)/shard_map/broadcast_in_dim | solution.py:50
  (15 shorter events, 0.0 us)
Async XLA Ops:
  0.0 1.6 copy-start
  58.4 2.7 copy-start.2
  64.0 53.4 %collective-permute-start = (bf16[1,512,2048]{2,1,0:T(8,128)(2,1)S(1)}, bf16[1,512,2048]{2,1,0:T(8,128)(2,1)S(1)}, u32[]{:S(2)}, u32[]{:S(2)}) collective-permute-start(bf16[1,512,2048]{2,1,0:T(8,128)(2,1)S(1)} %copy.23), channel_id=1, source_target_pairs={{0,1},{1,2},{2,3},{3,4},{4,5},{5,6},{6,7},{7,8},{8,9},{9,10},{10,1... | collective-permute-start | bytes 6291464 | tf_op jit(solution)/shard_map/ppermute | solution.py:13
  66.1 92.9 %collective-permute-start.3 = (bf16[1,512,2048]{2,1,0:T(8,128)(2,1)S(1)}, bf16[1,512,2048]{2,1,0:T(8,128)(2,1)S(1)}, u32[]{:S(2)}, u32[]{:S(2)}) collective-permute-start(bf16[1,512,2048]{2,1,0:T(8,128)(2,1)S(1)} %copy.23), channel_id=1, source_target_pairs={{1,0},{2,1},{3,2},{4,3},{5,4},{6,5},{7,6},{8,7},{9,8},{10,9},{11,1... | collective-permute-start | bytes 6291464 | tf_op jit(solution)/shard_map/ppermute | solution.py:13
  117.4 412.2 %copy-start.3 = (bf16[1,512,2048]{2,1,0:T(8,128)(2,1)}, bf16[1,512,2048]{2,1,0:T(8,128)(2,1)S(1)}, u32[]{:S(2)}) copy-start(bf16[1,512,2048]{2,1,0:T(8,128)(2,1)S(1)} %collective-permute-done) | copy-start | bytes 6291460
  159.1 370.6 %copy-start.4 = (bf16[1,512,2048]{2,1,0:T(8,128)(2,1)}, bf16[1,512,2048]{2,1,0:T(8,128)(2,1)S(1)}, u32[]{:S(2)}) copy-start(bf16[1,512,2048]{2,1,0:T(8,128)(2,1)S(1)} %collective-permute-done.3) | copy-start | bytes 6291460
  159.7 277.0 %collective-permute-start.1 = (bf16[2,512,2048]{2,1,0:T(8,128)(2,1)S(1)}, bf16[2,512,2048]{2,1,0:T(8,128)(2,1)S(1)}, u32[]{:S(2)}, u32[]{:S(2)}) collective-permute-start(bf16[2,512,2048]{2,1,0:T(8,128)(2,1)S(1)} %get-tuple-element.10), channel_id=1, source_target_pairs={{0,2},{1,3},{2,4},{3,5},{4,6},{5,7},{6,8},{7,9},{8,10},{9,11},{10,... | collective-permute-start | bytes 12582920 | tf_op jit(solution)/shard_map/ppermute | solution.py:13
  161.6 375.9 %copy-start.11 = (s32[1,15]{1,0:T(1,128)S(1)}, s32[1,15]{1,0:T(1,128)}, u32[]{:S(2)}) copy-start(s32[1,15]{1,0:T(1,128)} %param.8) | copy-start | bytes 184
  161.7 361.2 %collective-permute-start.4 = (bf16[2,512,2048]{2,1,0:T(8,128)(2,1)S(1)}, bf16[2,512,2048]{2,1,0:T(8,128)(2,1)S(1)}, u32[]{:S(2)}, u32[]{:S(2)}) collective-permute-start(bf16[2,512,2048]{2,1,0:T(8,128)(2,1)S(1)} %get-tuple-element.9), channel_id=1, source_target_pairs={{2,0},{3,1},{4,2},{5,3},{6,4},{7,5},{8,6},{9,7},{10,8},{11,9},{12,... | collective-permute-start | bytes 12582920 | tf_op jit(solution)/shard_map/ppermute | solution.py:13
  436.8 92.9 %copy-start.6 = (bf16[2,512,2048]{2,1,0:T(8,128)(2,1)}, bf16[2,512,2048]{2,1,0:T(8,128)(2,1)S(1)}, u32[]{:S(2)}) copy-start(bf16[2,512,2048]{2,1,0:T(8,128)(2,1)S(1)} %collective-permute-done.1) | copy-start | bytes 12582916
  522.9 7.1 copy-start.8
  529.9 17.0 %copy-start.10 = (f32[2048]{0:T(1024)S(1)}, f32[2048]{0:T(1024)}, u32[]{:S(2)}) copy-start(f32[2048]{0:T(1024)} %param.6) | copy-start | bytes 24580
  529.9 182.6 %collective-permute-start.2 = (bf16[4,512,2048]{2,1,0:T(8,128)(2,1)}, bf16[4,512,2048]{2,1,0:T(8,128)(2,1)}, u32[]{:S(2)}, u32[]{:S(2)}) collective-permute-start(bf16[4,512,2048]{2,1,0:T(8,128)(2,1)} %get-tuple-element.8), channel_id=1, source_target_pairs={{0,4},{1,5},{2,6},{3,7},{4,8},{5,9},{6,10},{7,11},{8,12},{9,13},{1... | collective-permute-start | bytes 25165832 | tf_op jit(solution)/shard_map/ppermute | solution.py:13
  532.0 199.0 %collective-permute-start.5 = (bf16[4,512,2048]{2,1,0:T(8,128)(2,1)}, bf16[4,512,2048]{2,1,0:T(8,128)(2,1)}, u32[]{:S(2)}, u32[]{:S(2)}) collective-permute-start(bf16[4,512,2048]{2,1,0:T(8,128)(2,1)} %get-tuple-element.7), channel_id=1, source_target_pairs={{4,0},{5,1},{6,2},{7,3},{8,4},{9,5},{10,6},{11,7},{12,8},{13,9},{1... | collective-permute-start | bytes 25165832 | tf_op jit(solution)/shard_map/ppermute | solution.py:13
  547.0 165.6 %copy-start.7 = (bf16[2,512,2048]{2,1,0:T(8,128)(2,1)S(1)}, bf16[2,512,2048]{2,1,0:T(8,128)(2,1)}, u32[]{:S(2)}) copy-start(bf16[2,512,2048]{2,1,0:T(8,128)(2,1)} %copy-done.6) | copy-start | bytes 12582916
  719.0 7.6 copy-start.5
  725.0 3.7 copy-start.9
  787.4 33.7 %copy-start.1 = (bf16[2048,512]{1,0:T(8,128)(2,1)S(1)}, bf16[2048,512]{1,0:T(8,128)(2,1)}, u32[]{:S(2)}) copy-start(bf16[2048,512]{1,0:T(8,128)(2,1)} %param.5) | copy-start | bytes 6291460
